TPU v7x, 32 devices: a whole 2x2x4 slice. The times are simulated.
32 devices in a mesh: member: 2 (over x), tm: 4 (over z), tile: 4 (over y, core).
Axes of the slice: x: 2, y: 2, z: 4, core: 2. Of those that a mesh axis runs over, the one named last changes fastest.
Arguments:
- flux: bfloat16 [64, 32, 16384], P(('member', 'tm'), 'tile'), parts along dimension 0, may hold values from -6 to 6
- footprint: bfloat16 [4, 256, 4, 16384], P('tm', 'tile'), may hold values from 1.4424324e-05 to 0.014404297
- foot_slot: int32 [4, 256, 4], P('tm', 'tile'), may hold values from 0 to 7
- wanted: int32 [4, 4, 4, 2], P('tm', 'tile'), may hold values from 0 to 127
- counts: int32 [4, 4, 4], P('tm', 'tile'), may hold values from 1 to 2
- observed: float32 [4, 256], P('tm', 'tile'), may hold values from -6 to 6
- inv_var: float32 [4, 256], P('tm', 'tile'), may hold values from 25.6 to 102.4
Outputs:
- modeled: float32 [8, 256], P(('member', 'tm'), 'tile'), parts along dimension 0
- gradient: float32 [64, 32, 16384], P(('member', 'tm'), 'tile'), parts along dimension 0
There are 2 independent parts, one for each index of `member`. A program takes and returns all parts, laid end to end along the dimension named above; an argument that names none is the same for every part. Nothing has to cross between parts.
All inputs are finite; a program needn't handle non-finite values.
Results may differ from a plain program's by a relative error of at most 0.0042.
Values may be sent and summed in bfloat16 or wider, within the bound.
A program may use at most 128 MiB of HBM per device.

v0:
```python
import jax
import jax.numpy as jnp
from jax import lax
from jax.sharding import PartitionSpec as P


def passed_along(value, axis, steps):
    count = lax.axis_size(axis)
    first, last = (max(0, -steps), min(count, count - steps))
    return lax.ppermute(value, axis, [(source, source + steps) for source in range(first, last)])


def on_device(flux, footprint, foot_slot, wanted, counts, observed, inv_var):
    steps_win, tiles_dev, cells = flux.shape
    owners = lax.axis_size("tile")
    capacity = wanted.shape[3]
    slots = owners * capacity
    own_rows = steps_win * tiles_dev
    own = flux.reshape(own_rows, cells)
    request = wanted.reshape(owners, capacity)
    served = lax.all_to_all(request, "tile", split_axis=0, concat_axis=0, tiled=True).reshape(slots)
    zero_half = jnp.zeros((), jnp.bfloat16)
    later = passed_along(served, "tm", -1)
    rows_now = jnp.where(
        (served >= own_rows)[:, None],
        jnp.take(own, jnp.maximum(served - own_rows, 0), axis=0),
        zero_half,
    )
    rows_later = jnp.where(
        (later < own_rows)[:, None],
        jnp.take(own, jnp.minimum(later, own_rows - 1), axis=0),
        zero_half,
    )
    outgoing = rows_now + passed_along(rows_later, "tm", 1)
    arrived_rows = lax.all_to_all(outgoing, "tile", split_axis=0, concat_axis=0, tiled=True)
    prints = footprint.reshape(-1, cells)
    scores = lax.dot_general(
        prints, arrived_rows, (((1,), (1,)), ((), ())), preferred_element_type=jnp.float32
    )
    entry = foot_slot.reshape(-1)
    slot_ids = jnp.arange(slots, dtype=jnp.int32)
    live_slot = slot_ids % capacity < jnp.repeat(counts.reshape(owners), capacity)
    select = (entry[:, None] == slot_ids[None, :]) & live_slot[None, :]
    entry_sums = jnp.sum(jnp.where(select, scores, 0.0), axis=1)
    soundings = observed.shape[1]
    per_sounding = foot_slot.shape[2]
    modeled = entry_sums.reshape(soundings, per_sounding).sum(axis=1)
    coef = ((modeled - observed[0]) * inv_var[0]).astype(jnp.bfloat16)
    spread = jnp.where(select, jnp.repeat(coef, per_sounding)[:, None], zero_half)
    adjoint = lax.dot_general(
        spread, prints, (((0,), (0,)), ((), ())), preferred_element_type=jnp.float32
    )
    returned_rows = lax.all_to_all(adjoint, "tile", split_axis=0, concat_axis=0, tiled=True)
    own_ids = jnp.arange(own_rows, dtype=jnp.int32)
    placing_now = ((served - own_rows)[:, None] == own_ids[None, :]).astype(jnp.float32)
    grad = lax.dot_general(
        placing_now,
        returned_rows,
        (((0,), (0,)), ((), ())),
        precision=lax.Precision.HIGHEST,
        preferred_element_type=jnp.float32,
    )
    back_past = jnp.where((served < own_rows)[:, None], returned_rows, 0.0)
    incoming = passed_along(back_past, "tm", -1)
    placing_later = (later[:, None] == own_ids[None, :]).astype(jnp.float32)
    grad = grad + lax.dot_general(
        placing_later,
        incoming,
        (((0,), (0,)), ((), ())),
        precision=lax.Precision.HIGHEST,
        preferred_element_type=jnp.float32,
    )
    return (modeled.reshape(1, soundings), grad.reshape(steps_win, tiles_dev, cells))


def solution(mesh):
    placed = (
        P(("member", "tm"), "tile", None),
        P("tm", "tile", None, None),
        P("tm", "tile", None),
        P("tm", "tile", None, None),
        P("tm", "tile", None),
        P("tm", "tile"),
        P("tm", "tile"),
    )
    return jax.shard_map(
        on_device,
        mesh=mesh,
        in_specs=placed,
        out_specs=(P(("member", "tm"), "tile"), P(("member", "tm"), "tile", None)),
        check_vma=False,
    )
```

profile of v0, /device:TPU:0, one launch (start us, length us, event | category | flops | bytes accessed | tf_op | source)
XLA Modules:
  0.0 101.6 jit_solution(3390461785795357767)
XLA Ops:
  0.6 1.5 %copy.18 = s32[4,1,2]{2,1,0:T(1,128)} copy(s32[4,1,2]{0,2,1:T(2,128)} %bitcast.28) | data formatting | bytes 64 | tf_op jit(solution)/shard_map/all_to_all | solution.py:21
  2.1 4.3 %all-to-all-start = ((s32[4,1,2]{2,1,0:T(1,128)}), s32[4,1,2]{2,1,0:T(1,128)S(1)}, u32[]{:S(2)}, u32[]{:S(2)}) async-start(s32[4,1,2]{2,1,0:T(1,128)} %copy.18), calls=%async_computation | async-start | bytes 4096 | tf_op jit(solution)/shard_map/all_to_all | solution.py:21
  6.4 12.6 %reshape.113 = bf16[256,16384]{1,0:T(8,128)(2,1)} reshape(bf16[1,64,4,16384]{3,2,1,0:T(4,128)(2,1)} %param.10) | data formatting | bytes 16777216 | tf_op jit(solution)/shard_map/reshape | solution.py:36
  19.0 12.6 %reshape.139 = bf16[256,16384,1]{1,0,2:T(8,128)(2,1)} reshape(bf16[1,64,4,16384]{3,2,1,0:T(4,128)(2,1)} %param.10) | data formatting | bytes 16777216 | tf_op jit(solution)/shard_map/reshape | solution.py:36
  31.6 0.1 eq.73
  32.0 0.1 copy.20
  32.2 0.5 broadcast.143
  32.7 0.7 reduce.3
  33.4 1.3 %collective-permute-start = (s32[8]{0:T(128)S(1)}, s32[8]{0:T(128)S(1)}, u32[]{:S(2)}, u32[]{:S(2)}) collective-permute-start(s32[8]{0:T(128)S(1)} %reshape.111), channel_id=1, source_target_pairs={{4,0},{8,4},{12,8},{5,1},{9,5},{13,9},{6,2},{10,6},{14,10},{7,3},{... | collective-permute-start | bytes 104 | tf_op jit(solution)/shard_map/ppermute | solution.py:10
  34.7 4.2 %collective-permute-done = s32[8]{0:T(128)S(1)} collective-permute-done((s32[8]{0:T(128)S(1)}, s32[8]{0:T(128)S(1)}, u32[]{:S(2)}, u32[]{:S(2)}) %collective-permute-start) | collective-permute-done | bytes 64 | tf_op jit(solution)/shard_map/ppermute | solution.py:10
  38.9 0.7 gather_fusion.1
  39.7 0.1 select_select_fusion
  39.8 3.9 %collective-permute-start.1 = (bf16[8,16384]{1,0:T(8,128)(2,1)S(1)}, bf16[8,16384]{1,0:T(8,128)(2,1)S(1)}, u32[]{:S(2)}, u32[]{:S(2)}) collective-permute-start(bf16[8,16384]{1,0:T(8,128)(2,1)S(1)} %select_select_fusion), channel_id=1, source_target_pairs={{0,4},{4,8},{8,12},{1,5},{5,9},{9,13},{2,6},{6,10},{10,14},{3,7},{... | collective-permute-start | bytes 786440 | tf_op jit(solution)/shard_map/ppermute | solution.py:10
  43.7 0.7 gather_fusion
  44.4 4.3 %collective-permute-done.1 = bf16[8,16384]{1,0:T(8,128)(2,1)S(1)} collective-permute-done((bf16[8,16384]{1,0:T(8,128)(2,1)S(1)}, bf16[8,16384]{1,0:T(8,128)(2,1)S(1)}, u32[]{:S(2)}, u32[]{:S(2)}) %collective-permute-start.1) | collective-permute-done | bytes 262176 | tf_op jit(solution)/shard_map/ppermute | solution.py:10
  48.7 0.1 fusion.3
  48.8 0.9 all_to_all.22
  49.7 3.4 %all-to-all-start.1 = ((bf16[4,2,16384]{2,1,0:T(2,128)(2,1)}), bf16[4,2,16384]{2,1,0:T(2,128)(2,1)S(1)}, u32[]{:S(2)}, u32[]{:S(2)}) async-start(bf16[4,2,16384]{2,1,0:T(2,128)(2,1)} %all_to_all.22), calls=%async_computation.1 | async-start | bytes 524288 | tf_op jit(solution)/shard_map/all_to_all | solution.py:35
  53.1 6.0 %all-to-all-done.1 = bf16[4,2,16384]{2,1,0:T(2,128)(2,1)S(1)} async-done(((bf16[4,2,16384]{2,1,0:T(2,128)(2,1)}), bf16[4,2,16384]{2,1,0:T(2,128)(2,1)S(1)}, u32[]{:S(2)}, u32[]{:S(2)}) %all-to-all-start.1) | async-done | bytes 262176 | tf_op jit(solution)/shard_map/all_to_all | solution.py:35
  59.1 0.1 all_to_all.24
  59.2 5.7 %fusion.2 = f32[256]{0:T(256)S(1)} fusion(bf16[8,16384]{1,0:T(8,128)(2,1)S(1)} %all_to_all.24, bf16[256,16384]{1,0:T(8,128)(2,1)} %reshape.113, s32[256]{0:T(256)S(1)} %eq.73, pred[8]{0:T(512)(128)(4,1)S(1)} %fusion.11), kind=kOutput, calls=%fused_computation.6 | convolution fusion | flops 67116800 | bytes 8652808 | tf_op jit(solution)/shard_map/dot_general | solution.py:37
  64.9 0.1 reshape.114
  65.0 0.1 reduce_sum.19
  65.2 0.1 broadcast_in_dim.78
  65.4 4.6 %fusion.5 = f32[4,2,16384]{2,1,0:T(2,128)S(1)} fusion(bf16[256,16384,1]{1,0,2:T(8,128)(2,1)} %reshape.139, bf16[4,2,256]{2,0,1:T(4,128)(2,1)S(1)} %and_select_fusion), kind=kOutput, calls=%fused_computation.16 | convolution fusion | flops 67108864 | bytes 8916992 | tf_op jit(solution)/shard_map/dot_general | solution.py:50
  70.0 11.2 %all_to_all.30 = f32[4,2,16384]{2,1,0:T(2,128)S(1)} all-to-all(f32[4,2,16384]{2,1,0:T(2,128)S(1)} %fusion.5), channel_id=1, replica_groups=mesh['member'=2,'tm'=4,'tile'=4] {'tile'}, dimensions={0} | all-to-all | bytes 1048576 | tf_op jit(solution)/shard_map/all_to_all | solution.py:53
  81.2 0.4 all_to_all.26
  81.6 0.1 broadcast_select_fusion
  81.7 1.3 %collective-permute-start.2 = (f32[8,16384]{1,0:T(8,128)S(1)}, f32[8,16384]{1,0:T(8,128)S(1)}, u32[]{:S(2)}, u32[]{:S(2)}) collective-permute-start(f32[8,16384]{1,0:T(8,128)S(1)} %broadcast_select_fusion), channel_id=1, source_target_pairs={{4,0},{8,4},{12,8},{5,1},{9,5},{13,9},{6,2},{10,6},{14,10},{7,3},{... | collective-permute-start | bytes 1572872 | tf_op jit(solution)/shard_map/ppermute | solution.py:10
  83.0 1.9 %fusion.7 = f32[64,16384]{1,0:T(8,128)S(1)} fusion(f32[8,16384]{1,0:T(8,128)S(1)} %all_to_all.26, s32[8]{0:T(128)S(1)} %get-tuple-element.8), kind=kOutput, calls=%fused_computation.20 | convolution fusion | flops 100663808 | bytes 4718624 | tf_op jit(solution)/shard_map/dot_general | solution.py:56
  84.9 12.7 %collective-permute-done.2 = f32[8,16384]{1,0:T(8,128)S(1)} collective-permute-done((f32[8,16384]{1,0:T(8,128)S(1)}, f32[8,16384]{1,0:T(8,128)S(1)}, u32[]{:S(2)}, u32[]{:S(2)}) %collective-permute-start.2) | collective-permute-done | bytes 524320 | tf_op jit(solution)/shard_map/ppermute | solution.py:10
  97.6 4.0 %fusion = f32[8,8,16384]{2,1,0:T(8,128)} fusion(f32[64,16384]{1,0:T(8,128)S(1)} %fusion.7, f32[8,16384]{1,0:T(8,128)S(1)} %collective-permute-done.2, s32[8]{0:T(128)S(1)} %collective-permute-done), kind=kOutput, calls=%fused_computation.3 | convolution fusion | flops 101712384 | bytes 8912928 | tf_op jit(solution)/shard_map/dot_general | solution.py:66
  (29 shorter events, 0.7 us)
Async XLA Ops:
  0.6 38.3 %copy-start = (bf16[8,8,16384]{2,1,0:T(8,128)(2,1)S(1)}, bf16[8,8,16384]{2,1,0:T(8,128)(2,1)}, u32[]{:S(2)}) copy-start(bf16[8,8,16384]{2,1,0:T(8,128)(2,1)} %param.9) | copy-start | bytes 6291460
  2.1 30.0 %all-to-all-start = ((s32[4,1,2]{2,1,0:T(1,128)}), s32[4,1,2]{2,1,0:T(1,128)S(1)}, u32[]{:S(2)}, u32[]{:S(2)}) async-start(s32[4,1,2]{2,1,0:T(1,128)} %copy.18), calls=%async_computation | async-start | bytes 4096 | tf_op jit(solution)/shard_map/all_to_all | solution.py:21
  19.0 12.6 %copy-start.2 = (s32[1,64,4]{1,2,0:T(4,128)S(1)}, s32[1,64,4]{1,2,0:T(4,128)}, u32[]{:S(2)}) copy-start(s32[1,64,4]{1,2,0:T(4,128)} %param.11) | copy-start | bytes 3076
  19.0 12.8 %copy-start.3 = (s32[1,1,4]{2,1,0:T(1,128)S(1)}, s32[1,1,4]{2,1,0:T(1,128)}, u32[]{:S(2)}) copy-start(s32[1,1,4]{2,1,0:T(1,128)} %param.13) | copy-start | bytes 52
  31.5 33.6 %copy-start.4 = (f32[1,64]{1,0:T(1,128)S(1)}, f32[1,64]{1,0:T(1,128)}, u32[]{:S(2)}) copy-start(f32[1,64]{1,0:T(1,128)} %param.15) | copy-start | bytes 772
  31.5 33.6 %copy-start.5 = (f32[1,64]{1,0:T(1,128)S(1)}, f32[1,64]{1,0:T(1,128)}, u32[]{:S(2)}) copy-start(f32[1,64]{1,0:T(1,128)} %param.14) | copy-start | bytes 772
  33.4 5.5 %collective-permute-start = (s32[8]{0:T(128)S(1)}, s32[8]{0:T(128)S(1)}, u32[]{:S(2)}, u32[]{:S(2)}) collective-permute-start(s32[8]{0:T(128)S(1)} %reshape.111), channel_id=1, source_target_pairs={{4,0},{8,4},{12,8},{5,1},{9,5},{13,9},{6,2},{10,6},{14,10},{7,3},{... | collective-permute-start | bytes 104 | tf_op jit(solution)/shard_map/ppermute | solution.py:10
  39.8 8.9 %collective-permute-start.1 = (bf16[8,16384]{1,0:T(8,128)(2,1)S(1)}, bf16[8,16384]{1,0:T(8,128)(2,1)S(1)}, u32[]{:S(2)}, u32[]{:S(2)}) collective-permute-start(bf16[8,16384]{1,0:T(8,128)(2,1)S(1)} %select_select_fusion), channel_id=1, source_target_pairs={{0,4},{4,8},{8,12},{1,5},{5,9},{9,13},{2,6},{6,10},{10,14},{3,7},{... | collective-permute-start | bytes 786440 | tf_op jit(solution)/shard_map/ppermute | solution.py:10
  49.7 9.4 %all-to-all-start.1 = ((bf16[4,2,16384]{2,1,0:T(2,128)(2,1)}), bf16[4,2,16384]{2,1,0:T(2,128)(2,1)S(1)}, u32[]{:S(2)}, u32[]{:S(2)}) async-start(bf16[4,2,16384]{2,1,0:T(2,128)(2,1)} %all_to_all.22), calls=%async_computation.1 | async-start | bytes 524288 | tf_op jit(solution)/shard_map/all_to_all | solution.py:35
  65.1 19.8 %copy-start.1 = (f32[64]{0:T(128)}, f32[64]{0:T(128)S(1)}, u32[]{:S(2)}) copy-start(f32[64]{0:T(128)S(1)} %reduce_sum.19) | copy-start | bytes 772
  81.7 15.9 %collective-permute-start.2 = (f32[8,16384]{1,0:T(8,128)S(1)}, f32[8,16384]{1,0:T(8,128)S(1)}, u32[]{:S(2)}, u32[]{:S(2)}) collective-permute-start(f32[8,16384]{1,0:T(8,128)S(1)} %broadcast_select_fusion), channel_id=1, source_target_pairs={{4,0},{8,4},{12,8},{5,1},{9,5},{13,9},{6,2},{10,6},{14,10},{7,3},{... | collective-permute-start | bytes 1572872 | tf_op jit(solution)/shard_map/ppermute | solution.py:10
where the time goes:
time: 103 us; the launch traced here: 102 us
  local copies, waits for them, and re-layouts  30.8 us (30%)
  waiting for transfers between devices  27.1 us (26%)
  matrix products  16.2 us (16%)
  starting transfers between devices  14.2 us (14%)
  blocking collectives  11.2 us (11%)
  other arithmetic  1.29 us (1%)
    reshape x2, local copies, waits for them, and re-layouts, on_device(): prints = footprint.reshape(-1, cells)  25.1 us
    ppermute x3, waiting for transfers between devices, passed_along(): lax.ppermute(value, axis, [(source, source + steps) for source in range(f...  21.1 us
    all_to_all x1, blocking collectives, on_device(): lax.all_to_all(adjoint, 'tile', split_axis=0, concat_axis=0, tiled=True)  11.2 us
    ppermute x3, starting transfers between devices, passed_along(): lax.ppermute(value, axis, [(source, source + steps) for source in range(f...  6.51 us
    all_to_all x1, waiting for transfers between devices, on_device(): lax.all_to_all(outgoing, 'tile', split_axis=0, concat_axis=0, tiled=True)  5.96 us
    dot_general x1, matrix products, on_device(): lax.dot_general(prints, arrived_rows, (((1,), (1,)), ((), ())), preferred...  5.67 us
    dot_general x1, matrix products, on_device(): lax.dot_general(spread, prints, (((0,), (0,)), ((), ())), preferred_eleme...  4.58 us
    all_to_all x1, starting transfers between devices, on_device(): lax.all_to_all(request, 'tile', split_axis=0, concat_axis=0, tiled=True)  4.26 us
  transfers between devices with their start and end apart: 5, of which 4 were waited for; matrix products, arithmetic and copies ran while one was open for 28% of the time, Pallas kernels for 0%

commit v1 on v0

v1 whole, which is shorter than its diff:
```python
import jax
import jax.numpy as jnp
from jax import lax
from jax.experimental import pallas as pl
from jax.experimental.pallas import tpu as pltpu
from jax.sharding import PartitionSpec as P

MESH = pl.DeviceIdType.MESH
LANES = 128
CHUNKS = 4
BLOCKS = 8


def exchange_kernel(
    own_hbm, prints_hbm, slots_ref, wanted_ref, counts_ref, observed_ref, inv_var_ref,
    modeled_ref, returned_ref, hot_ref,
    own_buf, prints_buf, send_buf, recv_buf, adj_buf, asks, asked, scores,
    own_sem, prints_sem, self_sem, ask_send, ask_recv, out_send, out_recv, back_send, back_recv,
):
    windows, owners = lax.axis_size("tm"), lax.axis_size("tile")
    win, me = lax.axis_index("tm"), lax.axis_index("tile")
    steps_win, groups, tiles_dev, _ = own_hbm.shape
    soundings, _, per_sounding, _ = prints_hbm.shape
    capacity = wanted_ref.shape[0]
    own_rows = steps_win * tiles_dev
    entries = soundings * per_sounding
    slots = owners * capacity
    rows = 2 * slots
    chunks = own_sem.shape[0]
    per_chunk = groups // chunks
    has_before, has_after = win > 0, win < windows - 1

    own_rows_view = own_buf.reshape(groups, own_rows, LANES)
    prints_view = prints_buf.reshape(groups, entries, LANES)
    send_view = send_buf.reshape(groups, rows, LANES)
    recv_view = recv_buf.reshape(groups, rows, LANES)
    adj_view = adj_buf.reshape(groups, slots, LANES)
    returned_view = returned_ref.reshape(groups, rows, LANES)

    def span(chunk):
        return pl.ds(chunk * per_chunk, per_chunk)

    def remote(source, target, send, recv, window, tile):
        return pltpu.make_async_remote_copy(
            src_ref=source, dst_ref=target, send_sem=send, recv_sem=recv,
            device_id={"tm": window, "tile": tile}, device_id_type=MESH,
        )

    def others(step):
        for away in range(1, owners):
            step(lax.rem(me + away, owners))

    @pl.loop(0, groups)
    def _(group):
        pltpu.make_async_copy(
            own_hbm.at[:, group], own_buf.at[group], own_sem.at[group // per_chunk]
        ).start()

    barrier = pltpu.get_barrier_semaphore()

    def greet(window, tile):
        pl.semaphore_signal(barrier, inc=1, device_id={"tm": window, "tile": tile}, device_id_type=MESH)

    others(lambda tile: greet(win, tile))

    @pl.when(has_before)
    def _():
        for tile in range(owners):
            greet(win - 1, tile)

    @pl.when(has_after)
    def _():
        for tile in range(owners):
            greet(win + 1, tile)

    row_id = lax.broadcasted_iota(jnp.int32, asks.shape[2:], 0)
    for tile in range(owners):
        for late in range(2):
            block = jnp.full(asks.shape[2:], -1, jnp.int32)
            for place in range(capacity):
                value = wanted_ref[place, tile] - (0 if late else own_rows)
                block = jnp.where(row_id == (late * owners + me) * capacity + place, value, block)
            asks[late, tile] = block

    @pl.loop(0, groups)
    def _(group):
        pltpu.make_async_copy(
            prints_hbm.at[:, group], prints_buf.at[group], prints_sem.at[group // per_chunk]
        ).start()

    near = lax.div(win + windows - 1, windows) + lax.div(2 * windows - 2 - win, windows)
    pl.semaphore_wait(barrier, owners - 1 + owners * near)

    def ask(late, tile):
        return remote(
            asks.at[late, tile], asked.at[late * owners + me],
            ask_send.at[late * owners + tile], ask_recv.at[late * owners + me], win - late, tile,
        )

    def ask_from(late, tile):
        return remote(
            asks.at[late, tile], asked.at[late * owners + tile],
            ask_send.at[late * owners + tile], ask_recv.at[late * owners + tile], win, me,
        )

    @pl.when(has_before)
    def _():
        for tile in range(owners):
            ask(1, tile).start()

    others(lambda tile: ask(0, tile).start())
    asked[me] = asks[0, me]

    @pl.when(jnp.logical_not(has_after))
    def _():
        asked[owners:] = jnp.full((owners,) + asked.shape[1:], -1, jnp.int32)

    @pl.when(jnp.logical_not(has_before))
    def _():
        @pl.loop(0, groups)
        def _(group):
            recv_buf[group, owners:] = jnp.zeros((owners, capacity, LANES), jnp.bfloat16)

    others(lambda tile: ask_from(0, tile).wait_recv())

    @pl.when(has_after)
    def _():
        for tile in range(owners):
            ask_from(1, tile).wait_recv()

    value = asked[0]
    for index in range(1, 2 * owners):
        value = jnp.maximum(value, asked[index])
    value = value[:, :own_rows]
    hot = (value == lax.broadcasted_iota(jnp.int32, value.shape, 1)).astype(jnp.float32).astype(jnp.bfloat16)
    hot_ref[...] = hot

    def out(chunk, late, tile):
        return remote(
            send_buf.at[span(chunk), late * owners + tile], recv_buf.at[span(chunk), late * owners + me],
            out_send.at[chunk, late * owners + tile], out_recv.at[chunk, late * owners + me], win + late, tile,
        )

    def out_from(chunk, late, tile):
        return remote(
            send_buf.at[span(chunk), late * owners + tile], recv_buf.at[span(chunk), late * owners + tile],
            out_send.at[chunk, late * owners + tile], out_recv.at[chunk, late * owners + tile], win, me,
        )

    def out_self(chunk):
        return pltpu.make_async_copy(
            send_buf.at[span(chunk), me], recv_buf.at[span(chunk), me], self_sem.at[0, chunk]
        )

    @pl.loop(0, chunks)
    def _(chunk):
        own_part = own_buf.at[span(chunk)]
        pltpu.make_async_copy(own_part, own_part, own_sem.at[chunk]).wait()

        @pl.loop(0, per_chunk // 2, unroll=4)
        def _(step):
            group = chunk * per_chunk + 2 * step
            pair = jnp.concatenate([own_rows_view[group], own_rows_view[group + 1]], axis=1)
            picked = jnp.dot(hot, pair, preferred_element_type=jnp.float32).astype(jnp.bfloat16)
            send_view[group] = picked[:, :LANES]
            send_view[group + 1] = picked[:, LANES:]

        @pl.when(has_after)
        def _():
            for tile in range(owners):
                out(chunk, 1, tile).start()

        others(lambda tile: out(chunk, 0, tile).start())
        out_self(chunk).start()

    scores[...] = jnp.zeros_like(scores)

    @pl.loop(0, chunks)
    def _(chunk):
        prints_part = prints_buf.at[span(chunk)]
        pltpu.make_async_copy(prints_part, prints_part, prints_sem.at[chunk]).wait()
        others(lambda tile: out_from(chunk, 0, tile).wait_recv())
        out_self(chunk).wait()

        @pl.when(has_before)
        def _():
            for tile in range(owners):
                out_from(chunk, 1, tile).wait_recv()

        def score(step, total):
            group = chunk * per_chunk + 2 * step
            pair = jnp.concatenate([prints_view[group], prints_view[group + 1]], axis=1)
            held = jnp.concatenate([recv_view[group], recv_view[group + 1]], axis=1)
            return total + lax.dot_general(
                held, pair, (((1,), (1,)), ((), ())), preferred_element_type=jnp.float32
            )

        scores[...] = lax.fori_loop(0, per_chunk // 2, score, scores[...], unroll=4)

    low = lax.broadcasted_iota(jnp.int32, (soundings, entries), 0) * per_sounding
    column = lax.broadcasted_iota(jnp.int32, (soundings, entries), 1)
    spread_of = ((column >= low) & (column < low + per_sounding)).astype(jnp.float32)
    each = jnp.dot(
        slots_ref[...].astype(jnp.float32), spread_of,
        precision=lax.Precision.HIGHEST, preferred_element_type=jnp.float32,
    )
    nth = lax.broadcasted_iota(jnp.int32, (per_sounding, entries), 0)
    at = lax.rem(lax.broadcasted_iota(jnp.int32, (per_sounding, entries), 1), per_sounding)
    entry = jnp.sum(jnp.where(nth == at, each, 0.0), axis=0, keepdims=True)
    slot_id = lax.broadcasted_iota(jnp.int32, (slots, entries), 0)
    have = jnp.zeros((slots, entries), jnp.int32)
    for tile in range(owners):
        have = jnp.where(slot_id // capacity == tile, counts_ref[0, tile], have)
    select = (slot_id.astype(jnp.float32) == entry) & (lax.rem(slot_id, capacity) < have)
    both = scores[:slots, :] + scores[slots:, :]
    entry_sums = jnp.sum(jnp.where(select, both, 0.0), axis=0, keepdims=True)
    modeled = lax.dot_general(
        jnp.broadcast_to(entry_sums, (8, entries)), spread_of, (((1,), (1,)), ((), ())),
        precision=lax.Precision.HIGHEST, preferred_element_type=jnp.float32,
    )
    modeled_ref[...] = modeled[:1]
    coef = ((modeled - observed_ref[...]) * inv_var_ref[...]).astype(jnp.bfloat16)
    coef_each = jnp.dot(coef, spread_of.astype(jnp.bfloat16), preferred_element_type=jnp.float32)[:1]
    weights = jnp.where(select, coef_each, 0.0).astype(jnp.bfloat16)

    def back(chunk, late, tile):
        return remote(
            adj_buf.at[span(chunk), tile], returned_ref.at[span(chunk), late * owners + me],
            back_send.at[chunk, late * owners + tile], back_recv.at[chunk, late * owners + me], win - late, tile,
        )

    def back_from(chunk, late, tile):
        return remote(
            adj_buf.at[span(chunk), tile], returned_ref.at[span(chunk), late * owners + tile],
            back_send.at[chunk, late * owners + tile], back_recv.at[chunk, late * owners + tile], win, me,
        )

    def back_self(chunk):
        return pltpu.make_async_copy(
            adj_buf.at[span(chunk), me], returned_ref.at[span(chunk), me], self_sem.at[1, chunk]
        )

    @pl.loop(0, chunks)
    def _(chunk):
        @pl.loop(0, per_chunk // 2, unroll=4)
        def _(step):
            group = chunk * per_chunk + 2 * step
            pair = jnp.concatenate([prints_view[group], prints_view[group + 1]], axis=1)
            adjoint = jnp.dot(weights, pair, preferred_element_type=jnp.float32).astype(jnp.bfloat16)
            adj_view[group] = adjoint[:, :LANES]
            adj_view[group + 1] = adjoint[:, LANES:]

        @pl.when(has_before)
        def _():
            for tile in range(owners):
                back(chunk, 1, tile).start()

        others(lambda tile: back(chunk, 0, tile).start())
        back_self(chunk).start()

    @pl.when(jnp.logical_not(has_after))
    def _():
        @pl.loop(0, groups)
        def _(group):
            returned_ref[group, owners:] = jnp.zeros((owners, capacity, LANES), jnp.bfloat16)

    others(lambda tile: ask(0, tile).wait_send())

    @pl.when(has_before)
    def _():
        for tile in range(owners):
            ask(1, tile).wait_send()

    @pl.loop(0, chunks)
    def _(chunk):
        others(lambda tile: out(chunk, 0, tile).wait_send())
        others(lambda tile: back(chunk, 0, tile).wait_send())
        others(lambda tile: back_from(chunk, 0, tile).wait_recv())
        back_self(chunk).wait()

        @pl.when(has_after)
        def _():
            for tile in range(owners):
                out(chunk, 1, tile).wait_send()
                back_from(chunk, 1, tile).wait_recv()

        @pl.when(has_before)
        def _():
            for tile in range(owners):
                back(chunk, 1, tile).wait_send()


def place_kernel(hot_ref, returned_ref, grad_ref):
    groups = returned_ref.shape[0]
    steps_win, tiles_dev, _ = grad_ref.shape
    rows = hot_ref.shape[0]
    view = returned_ref.reshape(groups, rows, LANES)
    hot = hot_ref[...]
    for group in range(0, groups, 2):
        pair = jnp.concatenate([view[group], view[group + 1]], axis=1)
        placed = lax.dot_general(
            hot, pair, (((0,), (0,)), ((), ())), preferred_element_type=jnp.float32
        )
        grad_ref[:, :, group * LANES:(group + 2) * LANES] = placed.reshape(steps_win, tiles_dev, 2 * LANES)


def on_device(flux, footprint, foot_slot, wanted, counts, observed, inv_var):
    steps_win, tiles_dev, cells = flux.shape
    _, soundings, per_sounding, _ = footprint.shape
    owners = lax.axis_size("tile")
    capacity = wanted.shape[3]
    own_rows = steps_win * tiles_dev
    entries = soundings * per_sounding
    groups = cells // LANES
    rows = 2 * owners * capacity
    wide = -(-own_rows // LANES) * LANES
    own = flux.reshape(steps_win, tiles_dev, groups, LANES).transpose(0, 2, 1, 3)
    prints = footprint.reshape(soundings, per_sounding, groups, LANES).transpose(0, 2, 1, 3)
    vmem = pl.BlockSpec(memory_space=pltpu.VMEM)
    smem = pl.BlockSpec(memory_space=pltpu.SMEM)
    hbm = pl.BlockSpec(memory_space=pl.ANY)
    dma = pltpu.SemaphoreType.DMA
    modeled, returned, hot = pl.pallas_call(
        exchange_kernel,
        out_shape=(
            jax.ShapeDtypeStruct((1, soundings), jnp.float32),
            jax.ShapeDtypeStruct((groups, 2 * owners, capacity, LANES), jnp.bfloat16),
            jax.ShapeDtypeStruct((rows, own_rows), jnp.bfloat16),
        ),
        in_specs=[hbm, hbm, vmem, smem, smem, vmem, vmem],
        out_specs=(vmem, vmem, vmem),
        scratch_shapes=[
            pltpu.VMEM((groups, steps_win, tiles_dev, LANES), jnp.bfloat16),
            pltpu.VMEM((groups, soundings, per_sounding, LANES), jnp.bfloat16),
            pltpu.VMEM((groups, 2 * owners, capacity, LANES), jnp.bfloat16),
            pltpu.VMEM((groups, 2 * owners, capacity, LANES), jnp.bfloat16),
            pltpu.VMEM((groups, owners, capacity, LANES), jnp.bfloat16),
            pltpu.VMEM((2, owners, rows, wide), jnp.int32),
            pltpu.VMEM((2 * owners, rows, wide), jnp.int32),
            pltpu.VMEM((rows, entries), jnp.float32),
            dma((CHUNKS,)),
            dma((CHUNKS,)),
            dma((2, CHUNKS)),
            dma((2 * owners,)),
            dma((2 * owners,)),
            dma((CHUNKS, 2 * owners)),
            dma((CHUNKS, 2 * owners)),
            dma((CHUNKS, 2 * owners)),
            dma((CHUNKS, 2 * owners)),
        ],
        compiler_params=pltpu.CompilerParams(collective_id=0, has_side_effects=True),
        name="exchange",
    )(
        own, prints, foot_slot[0].T, wanted[0, 0].T, counts[0], observed, inv_var,
    )
    per_block = groups // BLOCKS
    grad = pl.pallas_call(
        place_kernel,
        grid=(BLOCKS,),
        out_shape=jax.ShapeDtypeStruct((steps_win, tiles_dev, cells), jnp.float32),
        in_specs=[
            pl.BlockSpec((rows, own_rows), lambda block: (0, 0)),
            pl.BlockSpec((per_block, 2 * owners, capacity, LANES), lambda block: (block, 0, 0, 0)),
        ],
        out_specs=pl.BlockSpec((steps_win, tiles_dev, per_block * LANES), lambda block: (0, 0, block)),
        name="place",
    )(hot, returned)
    return modeled, grad


def solution(mesh):
    placed = (
        P(("member", "tm"), "tile", None),
        P("tm", "tile", None, None),
        P("tm", "tile", None),
        P("tm", "tile", None, None),
        P("tm", "tile", None),
        P("tm", "tile"),
        P("tm", "tile"),
    )
    return jax.shard_map(
        on_device,
        mesh=mesh,
        in_specs=placed,
        out_specs=(P(("member", "tm"), "tile"), P(("member", "tm"), "tile", None)),
        check_vma=False,
    )
```

time: 103 us -> 38.5 us (0.37)
  Pallas kernels: 0 us -> 36.8 us
  local copies, waits for them, and re-layouts: 30.8 us -> 0.51 us
  waiting for transfers between devices: 27.1 us -> 0 us
  matrix products: 16.2 us -> 0 us
  starting transfers between devices: 14.2 us -> 0 us
  blocking collectives: 11.2 us -> 0 us
  other arithmetic: 1.29 us -> 0 us
    pallas_call x0 -> x2, Pallas kernels: none -> 36.8 us  [the longest x1 30.7 us: on_device(): pl.pallas_call(exchange_kernel, out_shape=(jax.ShapeDtypeStruct((1, sound...]
    reshape x5 -> x0, local copies, waits for them, and re-layouts: 25.4 us -> none  [the longest x2 25.1 us: on_device(): prints = footprint.reshape(-1, cells)]
    ppermute x3 -> x0, waiting for transfers between devices: 21.1 us -> none  [passed_along(): lax.ppermute(value, axis, [(source, source + steps) for source in range(f...]
    dot_general x4 -> x0, matrix products: 16.2 us -> none  [the longest x1 5.67 us: on_device(): lax.dot_general(prints, arrived_rows, (((1,), (1,)), ((), ())), preferred...]
    all_to_all x1 -> x0, blocking collectives: 11.2 us -> none  [on_device(): lax.all_to_all(adjoint, 'tile', split_axis=0, concat_axis=0, tiled=True)]
    all_to_all x2 -> x0, starting transfers between devices: 7.67 us -> none  [the longest x1 4.26 us: on_device(): lax.all_to_all(request, 'tile', split_axis=0, concat_axis=0, tiled=True)]
    ppermute x3 -> x0, starting transfers between devices: 6.51 us -> none  [passed_along(): lax.ppermute(value, axis, [(source, source + steps) for source in range(f...]
    all_to_all x2 -> x0, waiting for transfers between devices: 5.96 us -> none  [the longest x1 5.96 us: on_device(): lax.all_to_all(outgoing, 'tile', split_axis=0, concat_axis=0, tiled=True)]
  transfers between devices with their start and end apart: 5 -> 0, of which waited for: 4 -> 0; matrix products, arithmetic and copies ran while one was open for 28% -> 0% of each run, Pallas kernels for 0% -> 0%
where the time goes in v1:
time: 38.5 us; the launch traced here: 38 us
  Pallas kernels  36.8 us (96%)
  between operations  0.65 us (2%)
  local copies, waits for them, and re-layouts  0.51 us (1%)
    pallas_call x1, Pallas kernels, on_device(): pl.pallas_call(exchange_kernel, out_shape=(jax.ShapeDtypeStruct((1, sound...  30.7 us
    pallas_call x1, Pallas kernels, on_device(): pl.pallas_call(place_kernel, grid=(BLOCKS,), out_shape=jax.ShapeDtypeStru...  6.15 us

profile of v1, /device:TPU:0, one launch (start us, length us, event | category | flops | bytes accessed | tf_op | source)
XLA Modules:
  0.0 38.0 jit_solution(14838967981365451801)
XLA Ops:
  0.6 30.7 %exchange.1 = (f32[1,64]{1,0:T(1,128)}, bf16[128,8,2,128]{3,2,1,0:T(2,128)(2,1)}, bf16[16,64]{1,0:T(8,128)(2,1)}) custom-call(bf16[8,128,8,128]{3,2,1,0:T(8,128)(2,1)} %bitcast.14, bf16[64,128,4,128]{3,2,1,0:T(4,128)(2,1)} %bitcast.13, s32[4,64]{1,0:T(4,128)} %bitcast.15, s32[2,4]{1,0:T(2,128)} %bitcast.16, s32[1,4]{1,0:T(1,128)} %bitcast.17, ...), custom_call_target="tpu_custom_call" | custom-call | tf_op jit(solution)/shard_map/exchange/pallas_call | solution.py:323
  31.3 0.0 copy-start
  31.3 6.2 %place.1 = f32[8,8,16384]{2,1,0:T(8,128)} custom-call(bf16[16,64]{1,0:T(8,128)(2,1)} %get-tuple-element.6.hot_ref, bf16[128,8,2,128]{3,2,1,0:T(2,128)(2,1)} %get-tuple-element.7.returned_ref), custom_call_target="tpu_custom_call" | custom-call | tf_op jit(solution)/shard_map/place/pallas_call | solution.py:357
  37.5 0.0 copy-done
  37.5 0.5 %copy.10 = f32[1,64]{1,0:T(1,128)} copy(f32[1,64]{1,0:T(1,128)S(1)} %copy-done) | data formatting | bytes 512
Async XLA Ops:
  31.3 6.2 %copy-start = (f32[1,64]{1,0:T(1,128)S(1)}, f32[1,64]{1,0:T(1,128)}, u32[]{:S(2)}) copy-start(f32[1,64]{1,0:T(1,128)} %get-tuple-element.10) | copy-start | bytes 772

commit v2 on v1

v2 whole, which is shorter than its diff:
```python
import jax
import jax.numpy as jnp
from jax import lax
from jax.experimental import pallas as pl
from jax.experimental.pallas import tpu as pltpu
from jax.sharding import PartitionSpec as P

MESH = pl.DeviceIdType.MESH
LANES = 128
OUT_SHARES = (2, 5, 5, 3, 1)
BACK_SHARES = (1, 3, 6, 6)
BLOCKS = 8


def spans(groups, shares):
    edges = [2 * (groups // 2 * sum(shares[:k]) // sum(shares)) for k in range(len(shares) + 1)]
    return [(low, high - low) for low, high in zip(edges, edges[1:])]


def exchange_kernel(
    own_hbm, prints_hbm, slots_ref, wanted_ref, counts_ref, observed_ref, inv_var_ref,
    modeled_ref, returned_ref, hot_ref,
    own_buf, prints_buf, send_buf, recv_buf, adj_buf, asks, asked, scores, mask, spread,
    own_sem, prints_sem, self_out, self_back, ask_send, ask_recv, out_send, out_recv, back_send, back_recv,
):
    windows, owners = lax.axis_size("tm"), lax.axis_size("tile")
    win, me = lax.axis_index("tm"), lax.axis_index("tile")
    steps_win, groups, tiles_dev, _ = own_hbm.shape
    soundings, _, per_sounding, _ = prints_hbm.shape
    capacity = wanted_ref.shape[0]
    own_rows = steps_win * tiles_dev
    entries = soundings * per_sounding
    slots = owners * capacity
    rows = 2 * slots
    out_parts, back_parts = spans(groups, OUT_SHARES), spans(groups, BACK_SHARES)
    has_before, has_after = win > 0, win < windows - 1

    own_rows_view = own_buf.reshape(groups, own_rows, LANES)
    prints_view = prints_buf.reshape(groups, entries, LANES)
    send_view = send_buf.reshape(groups, rows, LANES)
    recv_view = recv_buf.reshape(groups, rows, LANES)
    adj_view = adj_buf.reshape(groups, slots, LANES)
    returned_view = returned_ref.reshape(groups, rows, LANES)

    def out_span(chunk):
        return pl.ds(*out_parts[chunk])

    def back_span(chunk):
        return pl.ds(*back_parts[chunk])

    def load(source, target, semaphore):
        for chunk, (low, size) in enumerate(out_parts):
            @pl.loop(low, low + size)
            def _(group):
                pltpu.make_async_copy(source.at[:, group], target.at[group], semaphore.at[chunk]).start()

    def remote(source, target, send, recv, window, tile):
        return pltpu.make_async_remote_copy(
            src_ref=source, dst_ref=target, send_sem=send, recv_sem=recv,
            device_id={"tm": window, "tile": tile}, device_id_type=MESH,
        )

    def others(step):
        for away in range(1, owners):
            step(lax.rem(me + away, owners))

    barrier = pltpu.get_barrier_semaphore()

    def greet(window, tile):
        pl.semaphore_signal(barrier, inc=1, device_id={"tm": window, "tile": tile}, device_id_type=MESH)

    others(lambda tile: greet(win, tile))

    @pl.when(has_before)
    def _():
        for tile in range(owners):
            greet(win - 1, tile)

    @pl.when(has_after)
    def _():
        for tile in range(owners):
            greet(win + 1, tile)

    row_id = lax.broadcasted_iota(jnp.int32, asks.shape[2:], 0)
    for tile in range(owners):
        for late in range(2):
            block = jnp.full(asks.shape[2:], -1, jnp.int32)
            for place in range(capacity):
                value = wanted_ref[place, tile] - (0 if late else own_rows)
                block = jnp.where(row_id == (late * owners + me) * capacity + place, value, block)
            asks[late, tile] = block

    load(own_hbm, own_buf, own_sem)
    near = lax.div(win + windows - 1, windows) + lax.div(2 * windows - 2 - win, windows)
    pl.semaphore_wait(barrier, owners - 1 + owners * near)

    def ask(late, tile):
        return remote(
            asks.at[late, tile], asked.at[late * owners + me],
            ask_send.at[late * owners + tile], ask_recv.at[late * owners + me], win - late, tile,
        )

    def ask_from(late, tile):
        return remote(
            asks.at[late, tile], asked.at[late * owners + tile],
            ask_send.at[late * owners + tile], ask_recv.at[late * owners + tile], win, me,
        )

    @pl.when(has_before)
    def _():
        for tile in range(owners):
            ask(1, tile).start()

    others(lambda tile: ask(0, tile).start())
    asked[me] = asks[0, me]

    @pl.when(jnp.logical_not(has_after))
    def _():
        asked[owners:] = jnp.full((owners,) + asked.shape[1:], -1, jnp.int32)

    @pl.when(jnp.logical_not(has_before))
    def _():
        @pl.loop(0, groups)
        def _(group):
            recv_buf[group, owners:] = jnp.zeros((owners, capacity, LANES), jnp.bfloat16)

    load(prints_hbm, prints_buf, prints_sem)

    low = lax.broadcasted_iota(jnp.int32, (soundings, entries), 0) * per_sounding
    column = lax.broadcasted_iota(jnp.int32, (soundings, entries), 1)
    spread_of = ((column >= low) & (column < low + per_sounding)).astype(jnp.float32)
    spread[...] = spread_of
    each = jnp.dot(
        slots_ref[...].astype(jnp.float32), spread_of,
        precision=lax.Precision.HIGHEST, preferred_element_type=jnp.float32,
    )
    nth = lax.broadcasted_iota(jnp.int32, (per_sounding, entries), 0)
    at = lax.rem(lax.broadcasted_iota(jnp.int32, (per_sounding, entries), 1), per_sounding)
    entry = jnp.sum(jnp.where(nth == at, each, 0.0), axis=0, keepdims=True)
    slot_id = lax.broadcasted_iota(jnp.int32, (slots, entries), 0)
    have = jnp.zeros((slots, entries), jnp.int32)
    for tile in range(owners):
        have = jnp.where(slot_id // capacity == tile, counts_ref[0, tile], have)
    select = (slot_id.astype(jnp.float32) == entry) & (lax.rem(slot_id, capacity) < have)
    mask[...] = jnp.where(select, 1.0, 0.0)

    others(lambda tile: ask_from(0, tile).wait_recv())

    @pl.when(has_after)
    def _():
        for tile in range(owners):
            ask_from(1, tile).wait_recv()

    value = asked[0]
    for index in range(1, 2 * owners):
        value = jnp.maximum(value, asked[index])
    value = value[:, :own_rows]
    hot = (value == lax.broadcasted_iota(jnp.int32, value.shape, 1)).astype(jnp.float32).astype(jnp.bfloat16)
    hot_ref[...] = hot.astype(jnp.float32).T.astype(jnp.bfloat16)

    def out(chunk, late, tile):
        return remote(
            send_buf.at[out_span(chunk), late * owners + tile], recv_buf.at[out_span(chunk), late * owners + me],
            out_send.at[chunk, late * owners + tile], out_recv.at[chunk, late * owners + me], win + late, tile,
        )

    def out_from(chunk, late, tile):
        return remote(
            send_buf.at[out_span(chunk), late * owners + tile], recv_buf.at[out_span(chunk), late * owners + tile],
            out_send.at[chunk, late * owners + tile], out_recv.at[chunk, late * owners + tile], win, me,
        )

    def out_self(chunk):
        return pltpu.make_async_copy(
            send_buf.at[out_span(chunk), me], recv_buf.at[out_span(chunk), me], self_out.at[chunk]
        )

    for chunk, (low, size) in enumerate(out_parts):
        own_part = own_buf.at[out_span(chunk)]
        pltpu.make_async_copy(own_part, own_part, own_sem.at[chunk]).wait()

        @pl.loop(low // 2, (low + size) // 2, unroll=4)
        def _(step):
            group = 2 * step
            pair = jnp.concatenate([own_rows_view[group], own_rows_view[group + 1]], axis=1)
            picked = jnp.dot(hot, pair, preferred_element_type=jnp.float32).astype(jnp.bfloat16)
            send_view[group] = picked[:, :LANES]
            send_view[group + 1] = picked[:, LANES:]

        @pl.when(has_after)
        def _():
            for tile in range(owners):
                out(chunk, 1, tile).start()

        others(lambda tile: out(chunk, 0, tile).start())
        out_self(chunk).start()

    scores[...] = jnp.zeros_like(scores)

    for chunk, (low, size) in enumerate(out_parts):
        prints_part = prints_buf.at[out_span(chunk)]
        pltpu.make_async_copy(prints_part, prints_part, prints_sem.at[chunk]).wait()
        others(lambda tile: out_from(chunk, 0, tile).wait_recv())
        out_self(chunk).wait()

        @pl.when(has_before)
        def _():
            for tile in range(owners):
                out_from(chunk, 1, tile).wait_recv()

        def score(step, total):
            group = 2 * step
            pair = jnp.concatenate([prints_view[group], prints_view[group + 1]], axis=1)
            held = jnp.concatenate([recv_view[group], recv_view[group + 1]], axis=1)
            return total + lax.dot_general(
                held, pair, (((1,), (1,)), ((), ())), preferred_element_type=jnp.float32
            )

        scores[...] = lax.fori_loop(low // 2, (low + size) // 2, score, scores[...], unroll=4)

    select, spread_of = mask[...] > 0.0, spread[...]
    both = scores[:slots, :] + scores[slots:, :]
    entry_sums = jnp.sum(jnp.where(select, both, 0.0), axis=0, keepdims=True)
    modeled = lax.dot_general(
        jnp.broadcast_to(entry_sums, (8, entries)), spread_of, (((1,), (1,)), ((), ())),
        precision=lax.Precision.HIGHEST, preferred_element_type=jnp.float32,
    )
    modeled_ref[...] = modeled[:1]
    coef = ((modeled - observed_ref[...]) * inv_var_ref[...]).astype(jnp.bfloat16)
    coef_each = jnp.dot(coef, spread_of.astype(jnp.bfloat16), preferred_element_type=jnp.float32)[:1]
    weights = jnp.where(select, coef_each, 0.0).astype(jnp.bfloat16)

    def back(chunk, late, tile):
        return remote(
            adj_buf.at[back_span(chunk), tile], returned_ref.at[back_span(chunk), late * owners + me],
            back_send.at[chunk, late * owners + tile], back_recv.at[chunk, late * owners + me], win - late, tile,
        )

    def back_from(chunk, late, tile):
        return remote(
            adj_buf.at[back_span(chunk), tile], returned_ref.at[back_span(chunk), late * owners + tile],
            back_send.at[chunk, late * owners + tile], back_recv.at[chunk, late * owners + tile], win, me,
        )

    def back_self(chunk):
        return pltpu.make_async_copy(
            adj_buf.at[back_span(chunk), me], returned_ref.at[back_span(chunk), me], self_back.at[chunk]
        )

    for chunk, (low, size) in enumerate(back_parts):
        @pl.loop(low // 2, (low + size) // 2, unroll=4)
        def _(step):
            group = 2 * step
            pair = jnp.concatenate([prints_view[group], prints_view[group + 1]], axis=1)
            adjoint = jnp.dot(weights, pair, preferred_element_type=jnp.float32).astype(jnp.bfloat16)
            adj_view[group] = adjoint[:, :LANES]
            adj_view[group + 1] = adjoint[:, LANES:]

        @pl.when(has_before)
        def _():
            for tile in range(owners):
                back(chunk, 1, tile).start()

        others(lambda tile: back(chunk, 0, tile).start())
        back_self(chunk).start()

    @pl.when(jnp.logical_not(has_after))
    def _():
        @pl.loop(0, groups)
        def _(group):
            returned_ref[group, owners:] = jnp.zeros((owners, capacity, LANES), jnp.bfloat16)

    others(lambda tile: ask(0, tile).wait_send())

    @pl.when(has_before)
    def _():
        for tile in range(owners):
            ask(1, tile).wait_send()

    for chunk in range(len(out_parts)):
        others(lambda tile: out(chunk, 0, tile).wait_send())

        @pl.when(has_after)
        def _():
            for tile in range(owners):
                out(chunk, 1, tile).wait_send()

    for chunk in range(len(back_parts)):
        others(lambda tile: back(chunk, 0, tile).wait_send())
        others(lambda tile: back_from(chunk, 0, tile).wait_recv())
        back_self(chunk).wait()

        @pl.when(has_after)
        def _():
            for tile in range(owners):
                back_from(chunk, 1, tile).wait_recv()

        @pl.when(has_before)
        def _():
            for tile in range(owners):
                back(chunk, 1, tile).wait_send()


def place_kernel(hot_ref, returned_ref, modeled_ref, grad_hbm, modeled_out, grad_buf, grad_sem):
    groups = returned_ref.shape[0]
    steps_win, tiles_dev, _ = grad_buf.shape
    rows = hot_ref.shape[1]
    view = returned_ref.reshape(groups, rows, LANES)
    hot = hot_ref[...]
    modeled_out[...] = modeled_ref[...]
    copies = []
    for block, (low, size) in enumerate(spans(groups, (1,) * BLOCKS)):
        for group in range(low, low + size, 2):
            pair = jnp.concatenate([view[group], view[group + 1]], axis=1)
            placed = jnp.dot(hot, pair, preferred_element_type=jnp.float32)
            grad_buf[:, :, group * LANES:(group + 2) * LANES] = placed.reshape(steps_win, tiles_dev, 2 * LANES)
        cells = pl.ds(low * LANES, size * LANES)
        copies.append(pltpu.make_async_copy(grad_buf.at[:, :, cells], grad_hbm.at[:, :, cells], grad_sem.at[block]))
        copies[-1].start()
    for copy in copies:
        copy.wait()


def on_device(flux, footprint, foot_slot, wanted, counts, observed, inv_var):
    steps_win, tiles_dev, cells = flux.shape
    _, soundings, per_sounding, _ = footprint.shape
    owners = lax.axis_size("tile")
    capacity = wanted.shape[3]
    own_rows = steps_win * tiles_dev
    entries = soundings * per_sounding
    groups = cells // LANES
    rows = 2 * owners * capacity
    wide = -(-own_rows // LANES) * LANES
    own = flux.reshape(steps_win, tiles_dev, groups, LANES).transpose(0, 2, 1, 3)
    prints = footprint.reshape(soundings, per_sounding, groups, LANES).transpose(0, 2, 1, 3)
    vmem = pl.BlockSpec(memory_space=pltpu.VMEM)
    smem = pl.BlockSpec(memory_space=pltpu.SMEM)
    hbm = pl.BlockSpec(memory_space=pl.ANY)
    dma = pltpu.SemaphoreType.DMA
    modeled, returned, hot = pl.pallas_call(
        exchange_kernel,
        out_shape=(
            jax.ShapeDtypeStruct((1, soundings), jnp.float32),
            jax.ShapeDtypeStruct((groups, 2 * owners, capacity, LANES), jnp.bfloat16),
            jax.ShapeDtypeStruct((own_rows, rows), jnp.bfloat16),
        ),
        in_specs=[hbm, hbm, vmem, smem, smem, vmem, vmem],
        out_specs=(vmem, vmem, vmem),
        scratch_shapes=[
            pltpu.VMEM((groups, steps_win, tiles_dev, LANES), jnp.bfloat16),
            pltpu.VMEM((groups, soundings, per_sounding, LANES), jnp.bfloat16),
            pltpu.VMEM((groups, 2 * owners, capacity, LANES), jnp.bfloat16),
            pltpu.VMEM((groups, 2 * owners, capacity, LANES), jnp.bfloat16),
            pltpu.VMEM((groups, owners, capacity, LANES), jnp.bfloat16),
            pltpu.VMEM((2, owners, rows, wide), jnp.int32),
            pltpu.VMEM((2 * owners, rows, wide), jnp.int32),
            pltpu.VMEM((rows, entries), jnp.float32),
            pltpu.VMEM((owners * capacity, entries), jnp.float32),
            pltpu.VMEM((soundings, entries), jnp.float32),
            dma((len(OUT_SHARES),)),
            dma((len(OUT_SHARES),)),
            dma((len(OUT_SHARES),)),
            dma((len(BACK_SHARES),)),
            dma((2 * owners,)),
            dma((2 * owners,)),
            dma((len(OUT_SHARES), 2 * owners)),
            dma((len(OUT_SHARES), 2 * owners)),
            dma((len(BACK_SHARES), 2 * owners)),
            dma((len(BACK_SHARES), 2 * owners)),
        ],
        compiler_params=pltpu.CompilerParams(collective_id=0, has_side_effects=True),
        name="exchange",
    )(
        own, prints, foot_slot[0].T, wanted[0, 0].T, counts[0], observed, inv_var,
    )
    grad, modeled = pl.pallas_call(
        place_kernel,
        out_shape=(
            jax.ShapeDtypeStruct((steps_win, tiles_dev, cells), jnp.float32),
            jax.ShapeDtypeStruct((1, soundings), jnp.float32),
        ),
        in_specs=[vmem, vmem, vmem],
        out_specs=(hbm, vmem),
        scratch_shapes=[pltpu.VMEM((steps_win, tiles_dev, cells), jnp.float32), dma((BLOCKS,))],
        name="place",
    )(hot, returned, modeled)
    return modeled, grad


def solution(mesh):
    placed = (
        P(("member", "tm"), "tile", None),
        P("tm", "tile", None, None),
        P("tm", "tile", None),
        P("tm", "tile", None, None),
        P("tm", "tile", None),
        P("tm", "tile"),
        P("tm", "tile"),
    )
    return jax.shard_map(
        on_device,
        mesh=mesh,
        in_specs=placed,
        out_specs=(P(("member", "tm"), "tile"), P(("member", "tm"), "tile", None)),
        check_vma=False,
    )
```

time: 38.5 us -> 33.3 us (0.86)
  Pallas kernels: 36.8 us -> 32.5 us
  local copies, waits for them, and re-layouts: 0.51 us -> 0 us
    pallas_call x1, Pallas kernels: 6.15 us -> 3.83 us  [on_device(): pl.pallas_call(place_kernel, out_shape=(jax.ShapeDtypeStruct((steps_win,...]
    pallas_call x1, Pallas kernels: 30.7 us -> 28.7 us  [on_device(): pl.pallas_call(exchange_kernel, out_shape=(jax.ShapeDtypeStruct((1, sound...]
    unnamed x3 -> x0, local copies, waits for them, and re-layouts: 0.51 us -> none
where the time goes in v2:
time: 33.3 us; the launch traced here: 33.2 us
  Pallas kernels  32.5 us (98%)
  between operations  0.64 us (2%)
    pallas_call x1, Pallas kernels, on_device(): pl.pallas_call(exchange_kernel, out_shape=(jax.ShapeDtypeStruct((1, sound...  28.7 us
    pallas_call x1, Pallas kernels, on_device(): pl.pallas_call(place_kernel, out_shape=(jax.ShapeDtypeStruct((steps_win,...  3.83 us

profile of v2, /device:TPU:0, one launch (start us, length us, event | category | flops | bytes accessed | tf_op | source)
XLA Modules:
  0.0 33.2 jit_solution(11435594168219676979)
XLA Ops:
  0.6 28.7 %exchange.1 = (f32[1,64]{1,0:T(1,128)}, bf16[128,8,2,128]{3,2,1,0:T(2,128)(2,1)}, bf16[64,16]{1,0:T(8,128)(2,1)}) custom-call(bf16[8,128,8,128]{3,2,1,0:T(8,128)(2,1)} %bitcast.14, bf16[64,128,4,128]{3,2,1,0:T(4,128)(2,1)} %bitcast.13, s32[4,64]{1,0:T(4,128)} %bitcast.15, s32[2,4]{1,0:T(2,128)} %bitcast.16, s32[1,4]{1,0:T(1,128)} %bitcast.17, ...), custom_call_target="tpu_custom_call" | custom-call | tf_op jit(solution)/shard_map/exchange/pallas_call | solution.py:340
  29.3 3.8 %place.1 = (f32[8,8,16384]{2,1,0:T(8,128)}, f32[1,64]{1,0:T(1,128)}) custom-call(bf16[64,16]{1,0:T(8,128)(2,1)} %get-tuple-element.7.hot_ref, bf16[128,8,2,128]{3,2,1,0:T(2,128)(2,1)} %get-tuple-element.8.returned_ref, f32[1,64]{1,0:T(1,128)} %get-tuple-element.9.modeled_ref), custom_call_target="tpu_custom_call" | custom-call | tf_op jit(solution)/shard_map/place/pallas_call | solution.py:376

commit v3 on v2

--- a/solution.py
+++ b/solution.py
@@ -81,7 +81,7 @@
         for tile in range(owners):
             greet(win + 1, tile)
 
-    row_id = lax.broadcasted_iota(jnp.int32, asks.shape[2:], 0)
+    row_id = lax.broadcasted_iota(jnp.int32, asks.shape[2:], 1)
     for tile in range(owners):
         for late in range(2):
             block = jnp.full(asks.shape[2:], -1, jnp.int32)
@@ -154,9 +154,10 @@
     value = asked[0]
     for index in range(1, 2 * owners):
         value = jnp.maximum(value, asked[index])
-    value = value[:, :own_rows]
-    hot = (value == lax.broadcasted_iota(jnp.int32, value.shape, 1)).astype(jnp.float32).astype(jnp.bfloat16)
-    hot_ref[...] = hot.astype(jnp.float32).T.astype(jnp.bfloat16)
+    own_id = lax.broadcasted_iota(jnp.int32, (own_rows, rows), 0)
+    places = (value[:, :rows] == own_id).astype(jnp.float32)
+    hot_ref[...] = places.astype(jnp.bfloat16)
+    hot = places.T.astype(jnp.bfloat16)
 
     def out(chunk, late, tile):
         return remote(
@@ -179,7 +180,7 @@
         own_part = own_buf.at[out_span(chunk)]
         pltpu.make_async_copy(own_part, own_part, own_sem.at[chunk]).wait()
 
-        @pl.loop(low // 2, (low + size) // 2, unroll=4)
+        @pl.loop(low // 2, (low + size) // 2, unroll=size // 4)
         def _(step):
             group = 2 * step
             pair = jnp.concatenate([own_rows_view[group], own_rows_view[group + 1]], axis=1)
@@ -216,7 +217,7 @@
                 held, pair, (((1,), (1,)), ((), ())), preferred_element_type=jnp.float32
             )
 
-        scores[...] = lax.fori_loop(low // 2, (low + size) // 2, score, scores[...], unroll=4)
+        scores[...] = lax.fori_loop(low // 2, (low + size) // 2, score, scores[...], unroll=size // 4)
 
     select, spread_of = mask[...] > 0.0, spread[...]
     both = scores[:slots, :] + scores[slots:, :]
@@ -248,7 +249,7 @@
         )
 
     for chunk, (low, size) in enumerate(back_parts):
-        @pl.loop(low // 2, (low + size) // 2, unroll=4)
+        @pl.loop(low // 2, (low + size) // 2, unroll=size // 4)
         def _(step):
             group = 2 * step
             pair = jnp.concatenate([prints_view[group], prints_view[group + 1]], axis=1)
@@ -330,7 +331,7 @@
     entries = soundings * per_sounding
     groups = cells // LANES
     rows = 2 * owners * capacity
-    wide = -(-own_rows // LANES) * LANES
+    wide = -(-rows // LANES) * LANES
     own = flux.reshape(steps_win, tiles_dev, groups, LANES).transpose(0, 2, 1, 3)
     prints = footprint.reshape(soundings, per_sounding, groups, LANES).transpose(0, 2, 1, 3)
     vmem = pl.BlockSpec(memory_space=pltpu.VMEM)
@@ -352,8 +353,8 @@
             pltpu.VMEM((groups, 2 * owners, capacity, LANES), jnp.bfloat16),
             pltpu.VMEM((groups, 2 * owners, capacity, LANES), jnp.bfloat16),
             pltpu.VMEM((groups, owners, capacity, LANES), jnp.bfloat16),
-            pltpu.VMEM((2, owners, rows, wide), jnp.int32),
-            pltpu.VMEM((2 * owners, rows, wide), jnp.int32),
+            pltpu.VMEM((2, owners, 1, wide), jnp.int32),
+            pltpu.VMEM((2 * owners, 1, wide), jnp.int32),
             pltpu.VMEM((rows, entries), jnp.float32),
             pltpu.VMEM((owners * capacity, entries), jnp.float32),
             pltpu.VMEM((soundings, entries), jnp.float32),

time: 33.3 us -> 32.1 us (0.964)
  Pallas kernels: 32.5 us -> 31.3 us
    pallas_call x1, Pallas kernels: 28.7 us -> 27.5 us  [on_device(): pl.pallas_call(exchange_kernel, out_shape=(jax.ShapeDtypeStruct((1, sound...]
where the time goes in v3:
time: 32.1 us; the launch traced here: 32 us
  Pallas kernels  31.3 us (98%)
  between operations  0.64 us (2%)
    pallas_call x1, Pallas kernels, on_device(): pl.pallas_call(exchange_kernel, out_shape=(jax.ShapeDtypeStruct((1, sound...  27.5 us
    pallas_call x1, Pallas kernels, on_device(): pl.pallas_call(place_kernel, out_shape=(jax.ShapeDtypeStruct((steps_win,...  3.84 us

profile of v3, /device:TPU:0, one launch (start us, length us, event | category | flops | bytes accessed | tf_op | source)
XLA Modules:
  0.0 32.0 jit_solution(10369013870518123380)
XLA Ops:
  0.6 27.5 %exchange.1 = (f32[1,64]{1,0:T(1,128)}, bf16[128,8,2,128]{3,2,1,0:T(2,128)(2,1)}, bf16[64,16]{1,0:T(8,128)(2,1)}) custom-call(bf16[8,128,8,128]{3,2,1,0:T(8,128)(2,1)} %bitcast.14, bf16[64,128,4,128]{3,2,1,0:T(4,128)(2,1)} %bitcast.13, s32[4,64]{1,0:T(4,128)} %bitcast.15, s32[2,4]{1,0:T(2,128)} %bitcast.16, s32[1,4]{1,0:T(1,128)} %bitcast.17, ...), custom_call_target="tpu_custom_call" | custom-call | tf_op jit(solution)/shard_map/exchange/pallas_call | solution.py:341
  28.1 3.8 %place.1 = (f32[8,8,16384]{2,1,0:T(8,128)}, f32[1,64]{1,0:T(1,128)}) custom-call(bf16[64,16]{1,0:T(8,128)(2,1)} %get-tuple-element.7.hot_ref, bf16[128,8,2,128]{3,2,1,0:T(2,128)(2,1)} %get-tuple-element.8.returned_ref, f32[1,64]{1,0:T(1,128)} %get-tuple-element.9.modeled_ref), custom_call_target="tpu_custom_call" | custom-call | tf_op jit(solution)/shard_map/place/pallas_call | solution.py:377
